TPU v7x, 32 devices: a whole 2x2x4 slice. The times are simulated.
32 devices in a mesh: slides: 2 (over y), rows: 8 (over z, x), cols: 2 (over core).
Axes of the slice: x: 2, y: 2, z: 4, core: 2. Of those that a mesh axis runs over, the one named last changes fastest.
Arguments:
- tokens: bfloat16 [512, 32, 512], P(('slides', 'cols'), 'rows'), parts along dimension 0, may hold values from -6 to 6
- norm_gain: float32 [512], replicated, may hold values from 0.5 to 1.5
- w_in: bfloat16 [512, 2048], replicated, may hold values from -0.25 to 0.25
- w_bc: bfloat16 [512, 64], replicated, may hold values from -0.046875 to 0.046875
- rate_row: float32 [16, 1024], replicated, may hold values from 0.002 to 0.08
- rate_col: float32 [16, 1024], replicated, may hold values from 0.002 to 0.08
- skip_gain: float32 [1024], replicated, may hold values from 0.5 to 1.5
- w_out: bfloat16 [1024, 512], replicated, may hold values from -0.1875 to 0.1875
Outputs:
- mixed: bfloat16 [512, 32, 512], P(('slides', 'cols'), 'rows'), parts along dimension 0
There are 2 independent parts, one for each index of `slides`. A program takes and returns all parts, laid end to end along the dimension named above; an argument that names none is the same for every part. Nothing has to cross between parts.
All inputs are finite; a program needn't handle non-finite values.
Results may differ from a plain program's by a relative error of at most 0.013.
Values may be sent and summed in bfloat16 or wider, within the bound.
A program may use at most 64 MiB of HBM per device.

v0:
```python
import jax
import jax.numpy as jnp
from jax import lax
from jax.sharding import PartitionSpec as P


def prefix(shard, axis, combine, identity):
    size, here = (lax.axis_size(axis), lax.axis_index(axis))
    everything = jax.tree.map(
        lambda part, kind: lax.all_gather(part.astype(kind), axis),
        shard,
        (jnp.bfloat16, jnp.bfloat16),
    )
    start = jax.tree.map(
        lambda part, zero: jnp.broadcast_to(jnp.asarray(zero, part.dtype), part.shape),
        shard,
        identity,
    )

    def turn(k, before):
        reached = k < here
        new = combine(
            before, jax.tree.map(lambda part, own: part[k].astype(own.dtype), everything, shard)
        )
        return jax.tree.map(lambda a, b: jnp.where(reached, a, b), new, before)

    return lax.fori_loop(0, size, turn, start)


def block_scan(series, inject, readout, decay_factor, skip_weight, scan_axis):
    block_len = 16
    other_axis = 1 - scan_axis
    item_count = series.shape[other_axis]
    start_state = jnp.zeros((item_count, decay_factor.shape[0], decay_factor.shape[1]), jnp.float32)
    start_out = jnp.zeros(series.shape, jnp.float32)

    def one_block(block_id, carry):
        carried, outputs = carry
        first_row = block_id * block_len
        series_part = lax.dynamic_slice_in_dim(series, first_row, block_len, scan_axis).astype(
            jnp.float32
        )
        inject_part = lax.dynamic_slice_in_dim(inject, first_row, block_len, scan_axis).astype(
            jnp.float32
        )
        readout_part = lax.dynamic_slice_in_dim(readout, first_row, block_len, scan_axis).astype(
            jnp.float32
        )
        results = []
        for offset in range(block_len):
            value_now = lax.index_in_dim(series_part, offset, scan_axis, keepdims=False)
            inject_now = lax.index_in_dim(inject_part, offset, scan_axis, keepdims=False)
            read_now = lax.index_in_dim(readout_part, offset, scan_axis, keepdims=False)
            carried = decay_factor[None] * carried + inject_now[:, :, None] * value_now[:, None, :]
            results.append(
                jnp.einsum("ine,in->ie", carried, read_now, precision=lax.Precision.HIGHEST)
                + skip_weight * value_now
            )
        stacked = jnp.stack(results, axis=scan_axis)
        outputs = lax.dynamic_update_slice_in_dim(outputs, stacked, first_row, scan_axis)
        return (carried, outputs)

    carried, outputs = lax.fori_loop(
        0, series.shape[scan_axis] // block_len, one_block, (start_state, start_out)
    )
    return (outputs, carried)


def chain_join(earlier, later):
    return (earlier[0] * later[0], later[0][None] * earlier[1] + later[1])


def per_device(tokens, norm_gain, w_in, w_bc, rate_row, rate_col, skip_gain, w_out):
    inner_width = w_out.shape[0]
    state_width = rate_row.shape[0]
    as_float = tokens.astype(jnp.float32)
    scale_now = lax.rsqrt(jnp.mean(as_float * as_float, axis=-1, keepdims=True) + 1e-05)
    normed = (as_float * scale_now * norm_gain).astype(jnp.bfloat16)
    project = jnp.dot(normed, w_in, preferred_element_type=jnp.float32)
    inputs_u = project[..., :inner_width].astype(jnp.bfloat16)
    gate_z = project[..., inner_width:].astype(jnp.bfloat16)
    mixers = jnp.dot(normed, w_bc, preferred_element_type=jnp.float32).astype(jnp.bfloat16)
    col_vectors = mixers[..., 2 * state_width :]
    moved_u, moved_vectors = (
        lax.all_to_all(inputs_u, "rows", split_axis=0, concat_axis=1, tiled=True),
        lax.all_to_all(
            mixers[..., : 2 * state_width], "rows", split_axis=0, concat_axis=1, tiled=True
        ),
    )
    row_out, _ = block_scan(
        moved_u,
        moved_vectors[..., :state_width],
        moved_vectors[..., state_width:],
        jnp.exp(-rate_row),
        skip_gain,
        1,
    )
    row_mixed = row_out.astype(jnp.bfloat16)
    back_home = lax.all_to_all(row_mixed, "rows", split_axis=1, concat_axis=0, tiled=True)
    col_readout = col_vectors[..., state_width:]
    col_out, end_state = block_scan(
        back_home, col_vectors[..., :state_width], col_readout, jnp.exp(-rate_col), 1.0, 0
    )
    height = back_home.shape[0]
    total_decay = jnp.exp(-rate_col * height)
    incoming = prefix(
        (total_decay, end_state),
        "cols",
        chain_join,
        (jnp.ones_like(total_decay), jnp.zeros_like(end_state)),
    )[1]

    def correct(block_id, outputs):
        first_row = block_id * 16
        read_part = lax.dynamic_slice_in_dim(col_readout, first_row, 16, 0).astype(jnp.float32)
        steps_ahead = (first_row + 1 + jnp.arange(16, dtype=jnp.int32)).astype(jnp.float32)
        powers = jnp.exp(-rate_col[None] * steps_ahead[:, None, None])
        carried_part = jnp.einsum(
            "lwn,lne,wne->lwe", read_part, powers, incoming, precision=lax.Precision.HIGHEST
        )
        updated = lax.dynamic_slice_in_dim(outputs, first_row, 16, 0) + carried_part
        return lax.dynamic_update_slice_in_dim(outputs, updated, first_row, 0)

    col_out = lax.fori_loop(0, height // 16, correct, col_out)
    gated = (col_out * jax.nn.silu(gate_z.astype(jnp.float32))).astype(jnp.bfloat16)
    return jnp.dot(gated, w_out, preferred_element_type=jnp.float32).astype(jnp.bfloat16)


def solution(mesh):
    placed = (P(("slides", "cols"), "rows", None), P(), P(), P(), P(), P(), P(), P())
    return jax.shard_map(
        per_device,
        mesh=mesh,
        in_specs=placed,
        out_specs=P(("slides", "cols"), "rows", None),
        check_vma=False,
    )
```

profile of v0, /device:TPU:0, one launch (start us, length us, event | category | flops | bytes accessed | tf_op | source)
XLA Modules:
  0.0 232.9 jit_solution(4700963122558836914)
XLA Ops:
  0.0 1.5 fusion.184
  1.6 1.4 fusion.186
  5.0 7.3 %all-to-all-start = ((bf16[8,2,1024]{2,1,0:T(2,128)(2,1)}), bf16[8,2,1024]{2,1,0:T(2,128)(2,1)S(1)}, u32[]{:S(2)}, u32[]{:S(2)}) async-start(bf16[8,2,1024]{2,1,0:T(2,128)(2,1)} %reshape.149), calls=%async_computation | async-start | bytes 65536 | tf_op jit(solution)/shard_map/all_to_all | solution.py:86
  12.3 1.3 convolution_convert_fusion
  13.6 1.3 copy-done.5
  15.1 1.8 copy.78
  16.9 2.1 all-to-all-done
  19.0 3.8 %all-to-all-start.1 = ((bf16[128,4,1024]{2,1,0:T(4,128)(2,1)}), bf16[128,4,1024]{2,1,0:T(4,128)(2,1)S(1)}, u32[]{:S(2)}, u32[]{:S(2)}) async-start(bf16[128,4,1024]{2,1,0:T(4,128)(2,1)} %copy.78), calls=%async_computation.1 | async-start | bytes 2097152 | tf_op jit(solution)/shard_map/all_to_all | solution.py:85
  23.9 24.4 %all-to-all-done.1 = bf16[128,4,1024]{2,1,0:T(4,128)(2,1)S(1)} async-done(((bf16[128,4,1024]{2,1,0:T(4,128)(2,1)}), bf16[128,4,1024]{2,1,0:T(4,128)(2,1)S(1)}, u32[]{:S(2)}, u32[]{:S(2)}) %all-to-all-start.1) | async-done | bytes 1048608 | tf_op jit(solution)/shard_map/all_to_all | solution.py:85
  48.3 1.3 copy.79
  50.7 44.3 %while.62 = (s32[]{:T(128)}, f32[16,16,1024]{2,1,0:T(8,128)}, bf16[16,32,1024]{2,0,1:T(8,128)(2,1)}, f32[16,1024]{1,0:T(8,128)S(1)}, bf16[16,32,16]{2,0,1:T(8,12...) while((s32[]{:T(128)}, f32[16,16,1024]{2,1,0:T(8,128)}, ...), condition=%wide.region_2.0_spmd.clone, body=%wide.region_1.0_spmd.clone.sunk | while | flops 94638096 | bytes 42889080 | solution.py:63
  50.7 1.5 fusion.296
  52.2 1.2 dynamic-slice_convert_fusion.6
  54.1 1.4 fusion.297
  55.5 1.5 fusion.298
  60.3 1.3 fusion.302
  61.7 2.3 multiply_add_fusion.115
  72.3 1.5 fusion.296
  75.6 2.0 fusion.297
  77.7 2.0 fusion.298
  83.0 1.3 fusion.302
  84.4 2.3 multiply_add_fusion.115
  95.1 4.4 %all-to-all-start.2 = ((bf16[16,32,1024]{2,0,1:T(8,128)(2,1)}), bf16[16,32,1024]{2,0,1:T(8,128)(2,1)}, u32[]{:S(2)}, u32[]{:S(2)}) async-start(bf16[16,32,1024]{2,0,1:T(8,128)(2,1)} %get-tuple-element.491), calls=%async_computation.2 | async-start | bytes 2097152 | tf_op jit(solution)/shard_map/all_to_all | solution.py:99
  99.7 1.9 all-gather
  101.5 23.3 %all-to-all-done.2 = bf16[16,32,1024]{2,0,1:T(8,128)(2,1)} async-done(((bf16[16,32,1024]{2,0,1:T(8,128)(2,1)}), bf16[16,32,1024]{2,0,1:T(8,128)(2,1)}, u32[]{:S(2)}, u32[]{:S(2)}) %all-to-all-start.2) | async-done | bytes 1048608 | tf_op jit(solution)/shard_map/all_to_all | solution.py:99
  124.8 3.0 %copy.80 = bf16[16,8,4,1024]{3,2,0,1:T(4,128)(2,1)} copy(bf16[16,8,4,1024]{3,0,2,1:T(8,128)(2,1)} %bitcast.13) | data formatting | bytes 2097152 | tf_op jit(solution)/shard_map/all_to_all | solution.py:99
  127.9 1.8 broadcast_in_dim.18
  129.7 69.7 %while.63 = (s32[]{:T(128)}, f32[4,16,1024]{2,1,0:T(8,128)S(1)}, f32[128,4,1024]{2,1,0:T(4,128)}, f32[16,1024]{1,0:T(8,128)S(1)}, bf16[128,4,16]{0,2,1:T(8,128)(...) while((s32[]{:T(128)}, f32[4,16,1024]{2,1,0:T(8,128)S(1)}, ...), condition=%wide.region_4.0_spmd.clone, body=%wide.region_3.0_spmd.clone.sunk | while | flops 27526164 | bytes 9698083 | solution.py:63
  199.5 2.0 all-gather.1
  201.8 26.2 %while.61 = (s32[]{:T(128)}, f32[128,4,1024]{2,1,0:T(4,128)}, f32[1,16,1024]{2,1,0:T(8,128)S(1)}, bf16[128,4,16]{2,1,0:T(4,128)(2,1)S(1)}, f32[4,16,1024]{2,1,0:...) while((s32[]{:T(128)}, f32[128,4,1024]{2,1,0:T(4,128)}, f32[1,16,1024]{2,1,0:T(8,128)S(1)}, ...), condition=%wide.region_8.9_spmd, body=%wide.region_7.8_spmd.sunk | while | flops 3408935 | bytes 3483939 | solution.py:124
  202.1 1.3 multiply_reduce_fusion.2
  203.4 1.7 fusion.275
  205.4 1.3 multiply_reduce_fusion.2
  206.7 1.8 fusion.275
  208.6 1.3 multiply_reduce_fusion.2
  210.0 1.7 fusion.275
  211.9 1.3 multiply_reduce_fusion.2
  213.2 1.7 fusion.275
  215.2 1.3 multiply_reduce_fusion.2
  216.5 1.8 fusion.275
  218.5 1.3 multiply_reduce_fusion.2
  219.8 1.7 fusion.275
  221.7 1.3 multiply_reduce_fusion.2
  223.0 1.7 fusion.275
  225.0 1.3 multiply_reduce_fusion.2
  226.3 1.7 fusion.275
  228.0 3.7 %convolution_convert_fusion.1 = bf16[128,4,512]{2,0,1:T(8,128)(2,1)S(1)} fusion(bf16[1024,512]{1,0:T(8,128)(2,1)} %param.23, f32[128,4,1024]{2,1,0:T(4,128)} %get-tuple-element.495, bf16[128,4,2048]{2,0,1:T(8,128)(2,1)} %copy-done.5), kind=kOutput, calls=%fused_computation.390 | convolution fusion | flops 540803072 | bytes 4718592 | tf_op jit(solution)/shard_map/dot_general | solution.py:126
  231.7 1.2 copy.85
  (504 shorter events, 99.9 us)
Async XLA Ops:
  0.0 12.3 %copy-start = (bf16[512,2048]{1,0:T(8,128)(2,1)S(1)}, bf16[512,2048]{1,0:T(8,128)(2,1)}, u32[]{:S(2)}) copy-start(bf16[512,2048]{1,0:T(8,128)(2,1)} %param.18) | copy-start | bytes 6291460
  4.1 0.9 copy-start.17
  5.0 14.0 %all-to-all-start = ((bf16[8,2,1024]{2,1,0:T(2,128)(2,1)}), bf16[8,2,1024]{2,1,0:T(2,128)(2,1)S(1)}, u32[]{:S(2)}, u32[]{:S(2)}) async-start(bf16[8,2,1024]{2,1,0:T(2,128)(2,1)} %reshape.149), calls=%async_computation | async-start | bytes 65536 | tf_op jit(solution)/shard_map/all_to_all | solution.py:86
  13.6 1.4 copy-start.5
  15.1 7.8 %copy-start.16 = (f32[16,1024]{1,0:T(8,128)S(1)}, f32[16,1024]{1,0:T(8,128)}, u32[]{:S(2)}) copy-start(f32[16,1024]{1,0:T(8,128)} %param.20) | copy-start | bytes 196612
  19.0 29.3 %all-to-all-start.1 = ((bf16[128,4,1024]{2,1,0:T(4,128)(2,1)}), bf16[128,4,1024]{2,1,0:T(4,128)(2,1)S(1)}, u32[]{:S(2)}, u32[]{:S(2)}) async-start(bf16[128,4,1024]{2,1,0:T(4,128)(2,1)} %copy.78), calls=%async_computation.1 | async-start | bytes 2097152 | tf_op jit(solution)/shard_map/all_to_all | solution.py:85
  23.0 27.7 %copy-start.3 = (f32[1024]{0:T(1024)S(1)}, f32[1024]{0:T(1024)}, u32[]{:S(2)}) copy-start(f32[1024]{0:T(1024)} %param.22) | copy-start | bytes 12292
  54.1 3.0 %copy-start.1 = (f32[16,16,1024]{2,1,0:T(8,128)S(1)}, f32[16,16,1024]{2,1,0:T(8,128)}, u32[]{:S(2)}) copy-start(f32[16,16,1024]{2,1,0:T(8,128)} %get-tuple-element.1202) | copy-start | bytes 3145732 | tf_op jit(solution)/shard_map/while
  54.1 3.0 %copy-start.4 = (f32[16,16]{1,0:T(8,128)S(1)}, f32[16,16]{1,0:T(8,128)}, u32[]{:S(2)}) copy-start(f32[16,16]{1,0:T(8,128)} %get-tuple-element.1055) | copy-start | bytes 3076 | tf_op jit(solution)/shard_map/while
  54.1 3.0 %copy-start.14 = (bf16[16,16,1]{1,0,2:T(8,128)(2,1)S(1)}, bf16[16,16,1]{1,0,2:T(8,128)(2,1)}, u32[]{:S(2)}) copy-start(bf16[16,16,1]{1,0,2:T(8,128)(2,1)} %get-tuple-element.1058) | copy-start | bytes 1540 | tf_op jit(solution)/shard_map/while
  57.0 1.0 copy-start.13
  58.0 1.1 copy-start.12
  59.1 1.2 copy-start.11
  61.7 2.3 copy-start.10
  64.0 7.0 %copy-start.2 = (f32[16,16,1024]{2,1,0:T(8,128)}, f32[16,16,1024]{2,1,0:T(8,128)S(1)}, u32[]{:S(2)}) copy-start(f32[16,16,1024]{2,1,0:T(8,128)S(1)} %get-tuple-element.1229) | copy-start | bytes 3145732 | tf_op jit(solution)/shard_map/while
  64.0 1.0 copy-start.9
  65.0 0.9 copy-start.8
  65.9 1.5 copy-start.7
  66.7 1.6 copy-start.6
  75.6 4.1 %copy-start.1 = (f32[16,16,1024]{2,1,0:T(8,128)S(1)}, f32[16,16,1024]{2,1,0:T(8,128)}, u32[]{:S(2)}) copy-start(f32[16,16,1024]{2,1,0:T(8,128)} %get-tuple-element.1202) | copy-start | bytes 3145732 | tf_op jit(solution)/shard_map/while
  75.6 4.1 %copy-start.4 = (f32[16,16]{1,0:T(8,128)S(1)}, f32[16,16]{1,0:T(8,128)}, u32[]{:S(2)}) copy-start(f32[16,16]{1,0:T(8,128)} %get-tuple-element.1055) | copy-start | bytes 3076 | tf_op jit(solution)/shard_map/while
  75.6 4.1 %copy-start.14 = (bf16[16,16,1]{1,0,2:T(8,128)(2,1)S(1)}, bf16[16,16,1]{1,0,2:T(8,128)(2,1)}, u32[]{:S(2)}) copy-start(bf16[16,16,1]{1,0,2:T(8,128)(2,1)} %get-tuple-element.1058) | copy-start | bytes 1540 | tf_op jit(solution)/shard_map/while
  79.7 1.0 copy-start.13
  80.7 1.1 copy-start.12
  81.8 1.2 copy-start.11
  84.3 2.3 copy-start.10
  86.7 7.0 %copy-start.2 = (f32[16,16,1024]{2,1,0:T(8,128)}, f32[16,16,1024]{2,1,0:T(8,128)S(1)}, u32[]{:S(2)}) copy-start(f32[16,16,1024]{2,1,0:T(8,128)S(1)} %get-tuple-element.1229) | copy-start | bytes 3145732 | tf_op jit(solution)/shard_map/while
  86.7 1.0 copy-start.9
  87.7 0.9 copy-start.8
  88.6 1.5 copy-start.7
  89.4 1.6 copy-start.6
  95.0 4.4 %copy-start.18 = (bf16[128,4,64]{0,2,1:T(8,128)(2,1)S(1)}, bf16[128,4,64]{0,2,1:T(8,128)(2,1)}, u32[]{:S(2)}) copy-start(bf16[128,4,64]{0,2,1:T(8,128)(2,1)} %copy-done.17) | copy-start | bytes 196612
  95.0 4.6 %copy-start.15 = (f32[16,1024]{1,0:T(8,128)S(1)}, f32[16,1024]{1,0:T(8,128)}, u32[]{:S(2)}) copy-start(f32[16,1024]{1,0:T(8,128)} %param.21) | copy-start | bytes 196612
  95.1 29.8 %all-to-all-start.2 = ((bf16[16,32,1024]{2,0,1:T(8,128)(2,1)}), bf16[16,32,1024]{2,0,1:T(8,128)(2,1)}, u32[]{:S(2)}, u32[]{:S(2)}) async-start(bf16[16,32,1024]{2,0,1:T(8,128)(2,1)} %get-tuple-element.491), calls=%async_computation.2 | async-start | bytes 2097152 | tf_op jit(solution)/shard_map/all_to_all | solution.py:99
where the time goes:
time: 234 us; the launch traced here: 233 us
  matrix products  81.9 us (35%)
  other arithmetic  51.2 us (22%)
  waiting for transfers between devices  49.9 us (21%)
  local copies, waits for them, and re-layouts  27.4 us (12%)
  starting transfers between devices  15.5 us (7%)
  blocking collectives  3.85 us (2%)
  loops' own time  3.01 us (1%)
    dot_general x160, matrix products, one_block(): jnp.einsum('ine,in->ie', carried, read_now, precision=lax.Precision.HIGHEST)  75.8 us
    all_to_all x1, waiting for transfers between devices, per_device(): lax.all_to_all(inputs_u, 'rows', split_axis=0, concat_axis=1, tiled=True)  24.4 us
    all_to_all x1, waiting for transfers between devices, per_device(): lax.all_to_all(row_mixed, 'rows', split_axis=1, concat_axis=0, tiled=True)  23.3 us
    dynamic_update_slice x8, other arithmetic, correct(): return lax.dynamic_update_slice_in_dim(outputs, updated, first_row, 0)  13.9 us
    dot_general x8, other arithmetic, correct(): jnp.einsum('lwn,lne,wne->lwe', read_part, powers, incoming, precision=lax...  10.4 us
    convert_element_type x10, other arithmetic, one_block(): lax.dynamic_slice_in_dim(series, first_row, block_len, scan_axis)  9.74 us
    add x10, other arithmetic, one_block(): decay_factor[None] * carried  9.09 us
    dynamic_update_slice x10, local copies, waits for them, and re-layouts, one_block(): lax.dynamic_update_slice_in_dim(outputs, stacked, first_row, scan_axis)  7.58 us
  transfers between devices with their start and end apart: 3, of which 3 were waited for; matrix products, arithmetic and copies ran while one was open for 2% of the time, Pallas kernels for 0%

commit v1 on v0

v1 whole, which is shorter than its diff:
```python
import functools

import jax
import jax.numpy as jnp
from jax import lax
from jax.experimental import pallas as pl
from jax.experimental.pallas import tpu as pltpu
from jax.sharding import PartitionSpec as P

LANES = 128
VMEM_LIMIT = 56 * 1024 * 1024


def normalise(tokens, gain):
    as_float = tokens.astype(jnp.float32)
    scale_now = lax.rsqrt(jnp.mean(as_float * as_float, axis=-1, keepdims=True) + 1e-05)
    return (as_float * scale_now * gain).astype(jnp.bfloat16)


def spread_channels(ref, value, tiles):
    rows = value.shape[0]
    for t in range(tiles):
        ref[pl.ds(t, rows, stride=tiles), :] = value[:, t * LANES : (t + 1) * LANES]


def spread_vectors(ref, value, first, states):
    rows = value.shape[0]
    for n in range(states):
        ref[n, 0:rows, :] = jnp.broadcast_to(value[:, first + n : first + n + 1], (rows, LANES))


def scan_step(carried, decay, value, inject_ref, readout_ref, patch, start, tiles):
    new = []
    totals = [start, None]
    for n, state in enumerate(carried):
        inject = inject_ref[n, pl.ds(patch, tiles, stride=0), :]
        readout = readout_ref[n, pl.ds(patch, tiles, stride=0), :]
        state = decay[n] * state + inject * value
        term = readout * state
        totals[n % 2] = term if totals[n % 2] is None else totals[n % 2] + term
        new.append(state)
    return tuple(new), totals[0] + totals[1]


def row_kernel(states, items, steps, tok_ref, gain_ref, w_ref, wbc_ref, rate_ref, skip_ref,
               out_ref, u_ref, inject_ref, readout_ref, decay_ref, skip_tile):
    tiles = u_ref.shape[0] // tok_ref.shape[0]
    normed = normalise(tok_ref[...], gain_ref[...])
    mixers = jnp.dot(normed, wbc_ref[...], preferred_element_type=jnp.float32)
    mixers = mixers.astype(jnp.bfloat16).astype(jnp.float32)
    spread_vectors(inject_ref, mixers, 0, states)
    spread_vectors(readout_ref, mixers, states, states)
    width = 2 * LANES
    for k in range(tiles // 2):
        part = jnp.dot(normed, w_ref[:, k * width : (k + 1) * width],
                       preferred_element_type=jnp.float32)
        part = part.astype(jnp.bfloat16).astype(jnp.float32)
        for h in range(2):
            u_ref[pl.ds(2 * k + h, part.shape[0], stride=tiles), :] = part[:, h * LANES : (h + 1) * LANES]
    spread_channels(decay_ref, jnp.exp(-rate_ref[...]), tiles)
    spread_channels(skip_tile, skip_ref[...], tiles)
    decay = [decay_ref[n * tiles : (n + 1) * tiles, :] for n in range(states)]
    skip = skip_tile[...]
    group = 2 if items % 2 == 0 else 1
    zero = jnp.zeros((tiles, LANES), jnp.float32)

    def one_group(first, _):
        def one_step(j, carry):
            result = []
            for g in range(group):
                patch = (first * group + g) * steps + j
                value = u_ref[pl.ds(pl.multiple_of(patch * tiles, tiles), tiles), :]
                state, total = scan_step(carry[g], decay, value, inject_ref, readout_ref,
                                         patch, skip * value, tiles)
                out_ref[first * group + g, j] = total.astype(jnp.bfloat16)
                result.append(state)
            return tuple(result)

        lax.fori_loop(0, steps, one_step, tuple((zero,) * states for _ in range(group)))
        return 0

    lax.fori_loop(0, items // group, one_group, 0)


def row_stage(tok, gain, w_in, w_bc, rate, skip, inner):
    items, steps, width = tok.shape
    states = rate.shape[0]
    tiles = inner // LANES
    patches = items * steps
    whole = lambda *shape: pl.BlockSpec(shape, lambda i: (0,) * len(shape))
    return pl.pallas_call(
        functools.partial(row_kernel, states, items, steps),
        grid=(1,),
        in_specs=[
            whole(patches, width), whole(1, width), whole(width, inner),
            whole(width, w_bc.shape[1]), whole(states, inner), whole(1, inner),
        ],
        out_specs=whole(items, steps, tiles, LANES),
        out_shape=jax.ShapeDtypeStruct((items, steps, tiles, LANES), jnp.bfloat16),
        scratch_shapes=[
            pltpu.VMEM((patches * tiles, LANES), jnp.float32),
            pltpu.VMEM((states, patches + 8, LANES), jnp.float32),
            pltpu.VMEM((states, patches + 8, LANES), jnp.float32),
            pltpu.VMEM((states * tiles, LANES), jnp.float32),
            pltpu.VMEM((tiles, LANES), jnp.float32),
        ],
        compiler_params=pltpu.CompilerParams(vmem_limit_bytes=VMEM_LIMIT),
        name="row_stage",
    )(tok.reshape(patches, width), gain, w_in, w_bc, rate, skip)


def col_kernel(states, devices, cores, items, rm_ref, mix_ref, z_ref, rate_ref, wout_ref,
               out_ref, y_ref, inject_ref, readout_ref, decay_ref, gated_ref):
    tiles = rm_ref.shape[2]
    block = rm_ref.shape[0] // (devices * cores)
    mixers = mix_ref[...].astype(jnp.float32)
    spread_vectors(inject_ref, mixers, 0, states)
    spread_vectors(readout_ref, mixers, states, states)
    spread_channels(decay_ref, jnp.exp(-rate_ref[...]), tiles)
    decay = [decay_ref[n * tiles : (n + 1) * tiles, :] for n in range(states)]
    zero = jnp.zeros((tiles, LANES), jnp.float32)

    def one_block(k, carry):
        source = (k % devices * cores + k // devices) * block

        def one_step(s, carry):
            result = []
            for g in range(items):
                patch = (k * block + s) * items + g
                value = rm_ref[source + s, g].astype(jnp.float32)
                state, total = scan_step(carry[g], decay, value, inject_ref, readout_ref,
                                         patch, value, tiles)
                y_ref[pl.ds(pl.multiple_of(patch * tiles, tiles), tiles), :] = total
                result.append(state)
            return tuple(result)

        return lax.fori_loop(0, block, one_step, carry)

    lax.fori_loop(0, devices * cores, one_block, tuple((zero,) * states for _ in range(items)))
    patches = z_ref.shape[0]
    for t in range(tiles):
        gate = z_ref[:, t * LANES : (t + 1) * LANES].astype(jnp.float32)
        mixed = y_ref[pl.ds(t, patches, stride=tiles), :]
        gated_ref[:, t * LANES : (t + 1) * LANES] = (
            mixed * (gate / (1.0 + jnp.exp(-gate)))
        ).astype(jnp.bfloat16)
    out_ref[...] = jnp.dot(
        gated_ref[...], wout_ref[...], preferred_element_type=jnp.float32
    ).astype(jnp.bfloat16)


def col_stage(row_mixed, mixers, gate, rate, w_out, devices, cores):
    height, items, tiles, _ = row_mixed.shape
    states = rate.shape[0]
    patches = height * items
    inner, width = w_out.shape
    whole = lambda *shape: pl.BlockSpec(shape, lambda i: (0,) * len(shape))
    return pl.pallas_call(
        functools.partial(col_kernel, states, devices, cores, items),
        grid=(1,),
        in_specs=[
            whole(height, items, tiles, LANES), whole(patches, mixers.shape[1]),
            whole(patches, inner), whole(states, inner), whole(inner, width),
        ],
        out_specs=whole(patches, width),
        out_shape=jax.ShapeDtypeStruct((patches, width), jnp.bfloat16),
        scratch_shapes=[
            pltpu.VMEM((patches * tiles, LANES), jnp.float32),
            pltpu.VMEM((states, patches + 8, LANES), jnp.float32),
            pltpu.VMEM((states, patches + 8, LANES), jnp.float32),
            pltpu.VMEM((states * tiles, LANES), jnp.float32),
            pltpu.VMEM((patches, inner), jnp.bfloat16),
        ],
        compiler_params=pltpu.CompilerParams(vmem_limit_bytes=VMEM_LIMIT),
        name="col_stage",
    )(row_mixed, mixers, gate, rate, w_out)


def per_device(tokens, norm_gain, w_in, w_bc, rate_row, rate_col, skip_gain, w_out):
    inner = w_out.shape[0]
    states = rate_row.shape[0]
    width = tokens.shape[-1]
    devices, cores = lax.axis_size("rows"), lax.axis_size("cols")
    gain = norm_gain[None]
    by_row = lax.all_to_all(tokens, "rows", split_axis=0, concat_axis=1, tiled=True)
    by_col = lax.all_to_all(tokens, "cols", split_axis=1, concat_axis=0, tiled=True)
    row_mixed = row_stage(by_row, gain, w_in, w_bc, rate_row, skip_gain[None], inner)
    moved = lax.all_to_all(row_mixed, ("rows", "cols"), split_axis=1, concat_axis=0, tiled=True)
    normed = normalise(by_col.reshape(-1, width), gain)
    gate = jnp.dot(normed, w_in[:, inner:], preferred_element_type=jnp.float32).astype(jnp.bfloat16)
    mixers = jnp.dot(normed, w_bc[:, 2 * states :], preferred_element_type=jnp.float32).astype(jnp.bfloat16)
    mixed = col_stage(moved, mixers, gate, rate_col, w_out, devices, cores)
    mixed = mixed.reshape(by_col.shape[0], by_col.shape[1], -1)
    return lax.all_to_all(mixed, "cols", split_axis=0, concat_axis=1, tiled=True)


def solution(mesh):
    placed = (P(("slides", "cols"), "rows", None), P(), P(), P(), P(), P(), P(), P())
    return jax.shard_map(
        per_device,
        mesh=mesh,
        in_specs=placed,
        out_specs=P(("slides", "cols"), "rows", None),
        check_vma=False,
    )
```

time: 234 us -> 91.9 us (0.39)
  matrix products: 81.9 us -> 3.35 us
  other arithmetic: 51.2 us -> 0.18 us
  Pallas kernels: 0 us -> 26.2 us
  waiting for transfers between devices: 49.9 us -> 26.5 us
  local copies, waits for them, and re-layouts: 27.4 us -> 14.7 us
  loops' own time: 3.01 us -> 0 us
    dot_general x163 -> x2, matrix products: 81.9 us -> 3.35 us  [the longest x1 3 us: per_device(): jnp.dot(normed, w_in[:, inner:], preferred_element_type=jnp.float32)]
    pallas_call x0 -> x2, Pallas kernels: none -> 26.2 us  [the longest x1 13.5 us: col_stage(): pl.pallas_call(functools.partial(col_kernel, states, devices, cores, item...]
    all_to_all x3, waiting for transfers between devices: 49.9 us -> 26.5 us  [the longest x1 14.8 us: per_device(): lax.all_to_all(row_mixed, ('rows', 'cols'), split_axis=1, concat_axis=0,...]
    dynamic_update_slice x8 -> x0, other arithmetic: 13.9 us -> none  [correct(): return lax.dynamic_update_slice_in_dim(outputs, updated, first_row, 0)]
    convert_element_type x31 -> x0, other arithmetic: 11.3 us -> none  [the longest x10 9.74 us: one_block(): lax.dynamic_slice_in_dim(series, first_row, block_len, scan_axis)]
    dot_general x8 -> x0, other arithmetic: 10.4 us -> none  [correct(): jnp.einsum('lwn,lne,wne->lwe', read_part, powers, incoming, precision=lax...]
    add x10 -> x0, other arithmetic: 9.09 us -> none  [one_block(): decay_factor[None] * carried]
    dynamic_update_slice x10 -> x0, local copies, waits for them, and re-layouts: 7.58 us -> none  [one_block(): lax.dynamic_update_slice_in_dim(outputs, stacked, first_row, scan_axis)]
  transfers between devices with their start and end apart: 3 -> 3, of which waited for: 3 -> 2; matrix products, arithmetic and copies ran while one was open for 2% -> 16% of each run, Pallas kernels for 0% -> 14%
where the time goes in v1:
time: 91.9 us; the launch traced here: 90.1 us
  waiting for transfers between devices  26.5 us (29%)
  Pallas kernels  26.2 us (29%)
  local copies, waits for them, and re-layouts  14.7 us (16%)
  starting transfers between devices  14.7 us (16%)
  blocking collectives  4.36 us (5%)
  matrix products  3.35 us (4%)
    all_to_all x1, waiting for transfers between devices, per_device(): lax.all_to_all(row_mixed, ('rows', 'cols'), split_axis=1, concat_axis=0,...  14.8 us
    pallas_call x1, Pallas kernels, col_stage(): pl.pallas_call(functools.partial(col_kernel, states, devices, cores, item...  13.5 us
    pallas_call x1, Pallas kernels, row_stage(): pl.pallas_call(functools.partial(row_kernel, states, items, steps), grid=...  12.7 us
    all_to_all x1, waiting for transfers between devices, per_device(): lax.all_to_all(tokens, 'rows', split_axis=0, concat_axis=1, tiled=True)  11.8 us
    all_to_all x1, starting transfers between devices, per_device(): lax.all_to_all(tokens, 'rows', split_axis=0, concat_axis=1, tiled=True)  7.41 us
    all_to_all x1, blocking collectives, per_device(): lax.all_to_all(mixed, 'cols', split_axis=0, concat_axis=1, tiled=True)  4.36 us
    all_to_all x1, starting transfers between devices, per_device(): lax.all_to_all(row_mixed, ('rows', 'cols'), split_axis=1, concat_axis=0,...  3.84 us
    convert_element_type x2, local copies, waits for them, and re-layouts, normalise(): as_float = tokens.astype(jnp.float32)  3.51 us
  transfers between devices with their start and end apart: 3, of which 2 were waited for; matrix products, arithmetic and copies ran while one was open for 16% of the time, Pallas kernels for 14%

profile of v1, /device:TPU:0, one launch (start us, length us, event | category | flops | bytes accessed | tf_op | source)
XLA Modules:
  0.0 90.1 jit_solution(15714178036663484160)
XLA Ops:
  0.0 0.0 copy-start
  0.0 7.4 %all-to-all-start = ((bf16[128,4,512]{2,1,0:T(4,128)(2,1)}), bf16[128,4,512]{2,1,0:T(4,128)(2,1)S(1)}, u32[]{:S(2)}, u32[]{:S(2)}) async-start(bf16[128,4,512]{2,1,0:T(4,128)(2,1)} %param.8), calls=%async_computation | async-start | bytes 1048576 | tf_op jit(solution)/shard_map/all_to_all | solution.py:185
  7.4 2.0 %copy.36 = bf16[128,4,512]{2,0,1:T(8,128)(2,1)} copy(bf16[128,4,512]{2,1,0:T(4,128)(2,1)} %param.8) | data formatting | bytes 1048576 | tf_op args[0]
  9.4 0.0 copy-done
  9.4 0.7 copy.33.wbc_ref
  10.1 11.8 %all-to-all-done = bf16[128,4,512]{2,1,0:T(4,128)(2,1)S(1)} async-done(((bf16[128,4,512]{2,1,0:T(4,128)(2,1)}), bf16[128,4,512]{2,1,0:T(4,128)(2,1)S(1)}, u32[]{:S(2)}, u32[]{:S(2)}) %all-to-all-start) | async-done | bytes 524320 | tf_op jit(solution)/shard_map/all_to_all | solution.py:185
  21.9 3.5 %all-to-all-start.2 = ((bf16[128,4,512]{2,0,1:T(8,128)(2,1)}), bf16[128,4,512]{2,0,1:T(8,128)(2,1)S(1)}, u32[]{:S(2)}, u32[]{:S(2)}) async-start(bf16[128,4,512]{2,0,1:T(8,128)(2,1)} %copy.36), calls=%async_computation.2 | async-start | bytes 1048576 | tf_op jit(solution)/shard_map/all_to_all | solution.py:186
  25.4 0.2 copy.49
  25.6 0.9 %reshape.34.tok_ref = bf16[512,512]{1,0:T(8,128)(2,1)} reshape(bf16[16,8,4,512]{3,2,1,0:T(4,128)(2,1)S(1)} %bitcast.27) | data formatting | bytes 1048576 | tf_op jit(solution)/shard_map/reshape | solution.py:109
  26.6 12.7 %row_stage.1 = bf16[16,32,8,128]{3,2,1,0:T(8,128)(2,1)} custom-call(bf16[512,512]{1,0:T(8,128)(2,1)} %reshape.34.tok_ref, f32[1,512]{1,0:T(1,128)} %bitcast.30, bf16[512,2048]{1,0:T(8,128)(2,1)} %w_ref.1, bf16[512,64]{1,0:T(8,128)(2,1)} %copy.33.wbc_ref, f32[16,1024]{1,0:T(8,128)} %rate_ref.2, f32[1,1024]{1,0:T(1,128)} %bitcast.32), custom_call_target="tpu_custom_call" | custom-call | tf_op jit(solution)/shard_map/row_stage/pallas_call | solution.py:91
  39.3 2.5 %copy.34 = bf16[16,32,8,128]{3,2,0,1:T(8,128)(2,1)} copy(bf16[16,32,8,128]{3,2,1,0:T(8,128)(2,1)} %row_stage.1) | data formatting | bytes 2097152 | tf_op jit(solution)/shard_map/row_stage/pallas_call | solution.py:91
  41.8 0.0 all-to-all-done.2
  41.8 3.8 %all-to-all-start.1 = ((bf16[16,32,8,128]{3,2,0,1:T(8,128)(2,1)}), bf16[16,32,8,128]{3,2,0,1:T(8,128)(2,1)S(1)}, u32[]{:S(2)}, u32[]{:S(2)}) async-start(bf16[16,32,8,128]{3,2,0,1:T(8,128)(2,1)} %copy.34), calls=%async_computation.1 | async-start | bytes 2097152 | tf_op jit(solution)/shard_map/all_to_all | solution.py:188
  45.6 0.2 multiply_reduce_fusion
  45.8 0.0 copy-start.1
  45.8 0.1 copy.40
  46.0 0.1 rsqrt.12
  46.1 1.6 %copy.47 = f32[128,2,2,512]{3,2,0,1:T(2,128)} copy(bf16[128,2,2,512]{3,0,2,1:T(8,128)(2,1)S(1)} %bitcast.22) | data formatting | bytes 1572864 | tf_op jit(solution)/shard_map/convert_element_type | solution.py:15
  47.7 1.9 %reshape.36 = f32[512,512]{1,0:T(8,128)S(1)} reshape(f32[2,128,2,512]{3,2,1,0:T(2,128)} %bitcast.24) | data formatting | bytes 2097152 | tf_op jit(solution)/shard_map/convert_element_type | solution.py:15
  49.6 0.0 copy-done.1
  49.6 0.3 convolution_convert_fusion.1
  50.0 0.8 copy.41.mix_ref
  50.7 3.0 %convolution_convert_fusion.z_ref = bf16[512,1024]{1,0:T(8,128)(2,1)} fusion(bf16[512,2048]{1,0:T(8,128)(2,1)} %w_ref.1, f32[512,512]{1,0:T(8,128)S(1)} %reshape.36, f32[512]{0:T(512)S(1)} %copy-done.1, f32[512]{0:T(512)S(1)} %rsqrt.12), kind=kOutput, calls=%fused_computation | convolution fusion | flops 538181632 | bytes 3149824 | tf_op jit(solution)/shard_map/dot_general | solution.py:190
  53.7 14.8 %all-to-all-done.1 = bf16[16,32,8,128]{3,2,0,1:T(8,128)(2,1)S(1)} async-done(((bf16[16,32,8,128]{3,2,0,1:T(8,128)(2,1)}), bf16[16,32,8,128]{3,2,0,1:T(8,128)(2,1)S(1)}, u32[]{:S(2)}, u32[]{:S(2)}) %all-to-all-start.1) | async-done | bytes 1048608 | tf_op jit(solution)/shard_map/all_to_all | solution.py:188
  68.5 1.2 %copy.35 = bf16[16,16,2,8,128]{4,3,2,0,1:T(8,128)(2,1)} copy(bf16[16,16,2,8,128]{4,3,0,2,1:T(8,128)(2,1)S(1)} %bitcast.23) | data formatting | bytes 2097152 | tf_op jit(solution)/shard_map/all_to_all | solution.py:188
  69.7 13.5 %col_stage.1 = bf16[512,512]{1,0:T(8,128)(2,1)} custom-call(bf16[256,2,8,128]{3,2,1,0:T(8,128)(2,1)} %bitcast.25, bf16[512,32]{1,0:T(8,128)(2,1)} %copy.41.mix_ref, bf16[512,1024]{1,0:T(8,128)(2,1)} %convolution_convert_fusion.z_ref, f32[16,1024]{1,0:T(8,128)} %rate_ref.3, bf16[1024,512]{1,0:T(8,128)(2,1)} %wout_ref.1), custom_call_target="tpu_custom_call" | custom-call | tf_op jit(solution)/shard_map/col_stage/pallas_call | solution.py:158
  83.1 1.2 %reshape.35 = bf16[256,2,512]{2,1,0:T(2,128)(2,1)S(1)} reshape(bf16[512,512]{1,0:T(8,128)(2,1)} %col_stage.1) | data formatting | bytes 1048576 | tf_op jit(solution)/shard_map/reshape | solution.py:193
  84.4 4.4 %all_to_all.60 = bf16[256,2,512]{2,1,0:T(2,128)(2,1)S(1)} all-to-all(bf16[256,2,512]{2,1,0:T(2,128)(2,1)S(1)} %reshape.35), channel_id=1, replica_groups=mesh['slides'=2,'rows'=8,'cols'=2] {'cols'}, dimensions={0} | all-to-all | bytes 1048576 | tf_op jit(solution)/shard_map/all_to_all | solution.py:194
  88.7 0.4 copy.48
  89.1 1.0 %all_to_all.55 = bf16[128,4,512]{2,1,0:T(4,128)(2,1)} reshape(bf16[128,2,2,512]{3,2,1,0:T(2,128)(2,1)S(1)} %bitcast.29) | data formatting | bytes 1048576 | tf_op jit(solution)/shard_map/all_to_all | solution.py:194
  (1 shorter events, 0.0 us)
Async XLA Ops:
  0.0 9.4 %copy-start = (bf16[512,64]{0,1:T(8,128)(2,1)S(1)}, bf16[512,64]{0,1:T(8,128)(2,1)}, u32[]{:S(2)}) copy-start(bf16[512,64]{0,1:T(8,128)(2,1)} %param.11) | copy-start | bytes 196612
  0.0 21.9 %all-to-all-start = ((bf16[128,4,512]{2,1,0:T(4,128)(2,1)}), bf16[128,4,512]{2,1,0:T(4,128)(2,1)S(1)}, u32[]{:S(2)}, u32[]{:S(2)}) async-start(bf16[128,4,512]{2,1,0:T(4,128)(2,1)} %param.8), calls=%async_computation | async-start | bytes 1048576 | tf_op jit(solution)/shard_map/all_to_all | solution.py:185
  21.9 19.9 %all-to-all-start.2 = ((bf16[128,4,512]{2,0,1:T(8,128)(2,1)}), bf16[128,4,512]{2,0,1:T(8,128)(2,1)S(1)}, u32[]{:S(2)}, u32[]{:S(2)}) async-start(bf16[128,4,512]{2,0,1:T(8,128)(2,1)} %copy.36), calls=%async_computation.2 | async-start | bytes 1048576 | tf_op jit(solution)/shard_map/all_to_all | solution.py:186
  41.8 26.7 %all-to-all-start.1 = ((bf16[16,32,8,128]{3,2,0,1:T(8,128)(2,1)}), bf16[16,32,8,128]{3,2,0,1:T(8,128)(2,1)S(1)}, u32[]{:S(2)}, u32[]{:S(2)}) async-start(bf16[16,32,8,128]{3,2,0,1:T(8,128)(2,1)} %copy.34), calls=%async_computation.1 | async-start | bytes 2097152 | tf_op jit(solution)/shard_map/all_to_all | solution.py:188
  45.8 3.8 %copy-start.1 = (f32[512]{0:T(512)S(1)}, f32[512]{0:T(512)}, u32[]{:S(2)}) copy-start(f32[512]{0:T(512)} %param.9) | copy-start | bytes 6148

commit v2 on v1

v2 whole, which is shorter than its diff:
```python
import functools

import jax
import jax.numpy as jnp
from jax import lax
from jax.experimental import pallas as pl
from jax.experimental.pallas import tpu as pltpu
from jax.sharding import PartitionSpec as P

LANES = 128
VMEM_LIMIT = 60 * 1024 * 1024
MESH = pl.DeviceIdType.MESH


def normalise(tokens, gain):
    as_float = tokens.astype(jnp.float32)
    scale_now = lax.rsqrt(jnp.mean(as_float * as_float, axis=-1, keepdims=True) + 1e-05)
    return (as_float * scale_now * gain).astype(jnp.bfloat16)


def spread_channels(ref, value, tiles):
    rows = value.shape[0]
    for t in range(tiles):
        ref[pl.ds(t, rows, stride=tiles), :] = value[:, t * LANES : (t + 1) * LANES]


def spread_vectors(ref, value, first, states, base):
    rows = value.shape[0]
    for n in range(states):
        ref[n, pl.ds(base, rows), :] = jnp.broadcast_to(
            value[:, first + n : first + n + 1], (rows, LANES)
        )


def scan_step(carried, decay, value, inject_ref, readout_ref, patch, start, tiles):
    new = []
    totals = [start, None]
    for n, state in enumerate(carried):
        inject = inject_ref[n, pl.ds(patch, tiles, stride=0), :]
        readout = readout_ref[n, pl.ds(patch, tiles, stride=0), :]
        state = decay[n] * state + inject * value
        term = readout * state
        totals[n % 2] = term if totals[n % 2] is None else totals[n % 2] + term
        new.append(state)
    return tuple(new), totals[0] + totals[1]


def layer_kernel(
    states, rows_n, cols_n, share, per_core,
    tok_ref, gain_ref, win_ref, wbc_ref, rrate_ref, crate_ref, skip_ref, wout_ref,
    out_ref,
    tcol, tin, rsend, rrecv, u_ref, rb_ref, rc_ref, cb_ref, cc_ref, z_ref, y_ref, gated_ref,
    rdecay, cdecay, skip_tile, stage, land, state_ref,
    tsend_sem, tin_sem, csend_sem, crecv_sem, rsend_sem, rrecv_sem, osend_sem, orecv_sem,
):
    group_n = rows_n * cols_n
    pieces = tok_ref.shape[1]
    chunks = tin.shape[0]
    width = tok_ref.shape[3]
    inner = wout_ref.shape[0]
    tiles = inner // LANES
    piece_len = share * per_core
    chunk_len = group_n * piece_len
    blocks = stage.shape[0]
    blocks_home = blocks // cols_n
    block_len = stage.shape[1]
    r, c = lax.axis_index("rows"), lax.axis_index("cols")
    me = r * cols_n + c

    def spot(g):
        return {"rows": g // cols_n, "cols": g % cols_n}

    barrier = pltpu.get_barrier_semaphore()

    def greet(g, _):
        @pl.when(g != me)
        def _():
            pl.semaphore_signal(barrier, inc=1, device_id=spot(g), device_id_type=MESH)
        return 0

    lax.fori_loop(0, group_n, greet, 0)
    spread_channels(rdecay, jnp.exp(-rrate_ref[...]), tiles)
    spread_channels(cdecay, jnp.exp(-crate_ref[...]), tiles)
    spread_channels(skip_tile, skip_ref[...], tiles)
    pl.semaphore_wait(barrier, group_n - 1)

    local_chunks = max(1, chunks // cols_n)
    per_chunk = pieces // local_chunks

    def piece_of(k):
        piece = k // per_chunk * per_chunk + (k % per_chunk + me) % per_chunk
        place = c * pieces + piece
        return piece, place // group_n, place % group_n

    def token_copy(k):
        piece, q, g = piece_of(k)
        return g, pltpu.make_async_remote_copy(
            src_ref=tok_ref.at[:, piece], dst_ref=tin.at[q, r],
            send_sem=tsend_sem.at[piece], recv_sem=tin_sem.at[q],
            device_id=spot(g), device_id_type=MESH,
        )

    def send_tokens(k, _):
        piece, q, g = piece_of(k)

        @pl.when(g == me)
        def _():
            pltpu.make_async_copy(tok_ref.at[:, piece], tin.at[q, r], tin_sem.at[q]).start()

        @pl.when(g != me)
        def _():
            token_copy(k)[1].start()
        return 0

    lax.fori_loop(0, pieces, send_tokens, 0)

    def column_copy(step):
        other = (c + step) % cols_n
        return pltpu.make_async_remote_copy(
            src_ref=tok_ref.at[other], dst_ref=tcol.at[c],
            send_sem=csend_sem.at[step], recv_sem=crecv_sem.at[step],
            device_id={"cols": other}, device_id_type=MESH,
        )

    for step in range(1, cols_n):
        column_copy(step).start()

    def gate_part(tokens, core):
        normed = normalise(tokens.astype(jnp.float32).reshape(-1, width), gain_ref[...])
        count = normed.shape[0]
        base = pl.multiple_of(core * count, count)
        mixers = jnp.dot(normed, wbc_ref[...], preferred_element_type=jnp.float32)
        mixers = mixers.astype(jnp.bfloat16).astype(jnp.float32)
        spread_vectors(cb_ref, mixers, 2 * states, states, base)
        spread_vectors(cc_ref, mixers, 3 * states, states, base)
        for k in range(0, inner, 2 * LANES):
            z_ref[pl.ds(base, count), k : k + 2 * LANES] = jnp.dot(
                normed, win_ref[:, inner + k : inner + k + 2 * LANES],
                preferred_element_type=jnp.float32,
            ).astype(jnp.bfloat16)

    gate_part(tok_ref[c], c)

    zero = jnp.zeros((tiles, LANES), jnp.float32)
    lanes = 2 if share % 2 == 0 else 1

    def result_copy(q, k):
        g = (me + k) % group_n
        return pltpu.make_async_remote_copy(
            src_ref=rsend.at[q, pl.ds(g * piece_len, piece_len)],
            dst_ref=rrecv.at[q, pl.ds(me * piece_len, piece_len)],
            send_sem=rsend_sem.at[q, k], recv_sem=rrecv_sem.at[q],
            device_id=spot(g), device_id_type=MESH,
        )

    def row_chunk(q, _):
        pltpu.make_async_copy(tin.at[q], tin.at[q], tin_sem.at[q]).wait()
        normed = normalise(tin[q].astype(jnp.float32).reshape(chunk_len, width), gain_ref[...])
        mixers = jnp.dot(normed, wbc_ref[...], preferred_element_type=jnp.float32)
        mixers = mixers.astype(jnp.bfloat16).astype(jnp.float32)
        spread_vectors(rb_ref, mixers, 0, states, 0)
        spread_vectors(rc_ref, mixers, states, states, 0)
        for k in range(0, tiles, 2):
            part = jnp.dot(normed, win_ref[:, k * LANES : (k + 2) * LANES],
                           preferred_element_type=jnp.float32)
            part = part.astype(jnp.bfloat16).astype(jnp.float32)
            for h in range(2):
                u_ref[pl.ds(k + h, chunk_len, stride=tiles), :] = part[:, h * LANES : (h + 1) * LANES]
        decay = [rdecay[n * tiles : (n + 1) * tiles, :] for n in range(states)]
        skip = skip_tile[...]

        def one_group(first, _):
            def one_step(j, carry):
                carry = list(carry)
                for w in range(per_core):
                    for b in range(lanes):
                        patch = (j * share + first * lanes + b) * per_core + w
                        value = u_ref[pl.ds(pl.multiple_of(patch * tiles, tiles), tiles), :]
                        carry[b], total = scan_step(carry[b], decay, value, rb_ref, rc_ref,
                                                    patch, skip * value, tiles)
                        rsend[q, patch] = total.astype(jnp.bfloat16)
                return tuple(carry)

            lax.fori_loop(0, group_n, one_step, tuple((zero,) * states for _ in range(lanes)))
            return 0

        lax.fori_loop(0, share // lanes, one_group, 0)

        def send_result(k, _):
            result_copy(q, k).start()
            return 0

        pltpu.make_async_copy(
            rsend.at[q, pl.ds(me * piece_len, piece_len)],
            rrecv.at[q, pl.ds(me * piece_len, piece_len)], rrecv_sem.at[q],
        ).start()
        lax.fori_loop(1, group_n, send_result, 0)
        return 0

    lax.fori_loop(0, chunks, row_chunk, 0)

    for step in range(1, cols_n):
        column_copy(step).wait_recv()
        source = (c + cols_n - step) % cols_n
        gate_part(tcol[source], source)

    for g in range(per_core):
        for n in range(states):
            state_ref[g, n] = zero

    def out_copy(o):
        return pltpu.make_async_remote_copy(
            src_ref=stage.at[o], dst_ref=land.at[c, o % blocks_home],
            send_sem=osend_sem.at[o], recv_sem=orecv_sem.at[c, o % blocks_home],
            device_id={"cols": o // blocks_home}, device_id_type=MESH,
        )

    def col_chunk(q, _):
        pltpu.make_async_copy(rrecv.at[q], rrecv.at[q], rrecv_sem.at[q]).wait()
        decay = [cdecay[n * tiles : (n + 1) * tiles, :] for n in range(states)]
        base = q * chunk_len

        def one_step(s, carry):
            result = []
            for g in range(per_core):
                patch = s * per_core + g
                value = rrecv[q, patch].astype(jnp.float32)
                state, total = scan_step(carry[g], decay, value, cb_ref, cc_ref,
                                         base + patch, value, tiles)
                y_ref[pl.ds(pl.multiple_of(patch * tiles, tiles), tiles), :] = total
                result.append(state)
            return tuple(result)

        carry = tuple(tuple(state_ref[g, n] for n in range(states)) for g in range(per_core))
        carry = lax.fori_loop(0, chunk_len // per_core, one_step, carry)
        for g in range(per_core):
            for n in range(states):
                state_ref[g, n] = carry[g][n]
        start = pl.multiple_of(base, chunk_len)
        for t in range(tiles):
            gate = z_ref[pl.ds(start, chunk_len), t * LANES : (t + 1) * LANES].astype(jnp.float32)
            mixed = y_ref[pl.ds(t, chunk_len, stride=tiles), :]
            gated_ref[:, t * LANES : (t + 1) * LANES] = (
                mixed * (gate / (1.0 + jnp.exp(-gate)))
            ).astype(jnp.bfloat16)
        result = jnp.dot(gated_ref[...], wout_ref[...], preferred_element_type=jnp.float32)
        result = result.astype(jnp.bfloat16)
        for k in range(blocks // chunks):
            o = q * (blocks // chunks) + k
            block = result[k * block_len : (k + 1) * block_len]
            stage[o] = block

            @pl.when(o // blocks_home == c)
            def _():
                land[c, o % blocks_home] = block

            @pl.when(o // blocks_home != c)
            def _():
                out_copy(o).start()
        return 0

    lax.fori_loop(0, chunks, col_chunk, 0)

    def drain_tokens(k, _):
        g, copy = token_copy(k)

        @pl.when(g != me)
        def _():
            copy.wait_send()
        return 0

    lax.fori_loop(0, pieces, drain_tokens, 0)
    for step in range(1, cols_n):
        column_copy(step).wait_send()

    def drain_results(q, _):
        def one(k, _):
            result_copy(q, k).wait_send()
            return 0
        return lax.fori_loop(1, group_n, one, 0)

    lax.fori_loop(0, chunks, drain_results, 0)

    def drain_out(o, _):
        @pl.when(o // blocks_home != c)
        def _():
            out_copy(o).wait_send()
        return 0

    lax.fori_loop(0, blocks, drain_out, 0)
    for source in range(cols_n):
        @pl.when(source != c)
        def _():
            for i in range(blocks_home):
                pltpu.make_async_copy(
                    land.at[source, i], land.at[source, i], orecv_sem.at[source, i]
                ).wait()
    out_ref[...] = land[...]


def per_device(tokens, norm_gain, w_in, w_bc, rate_row, rate_col, skip_gain, w_out):
    inner, width_out = w_out.shape
    states = rate_row.shape[0]
    height, columns, width = tokens.shape
    rows_n, cols_n = lax.axis_size("rows"), lax.axis_size("cols")
    group_n = rows_n * cols_n
    per_core = columns // cols_n
    total = height * cols_n
    share = min(4, total // group_n)
    chunks = total // (group_n * share)
    pieces = height // share
    piece_len = share * per_core
    chunk_len = group_n * piece_len
    tiles = inner // LANES
    blocks = max(chunks, cols_n)
    block_len = total * per_core // blocks
    patches = total * per_core
    arranged = tokens.reshape(height, cols_n, per_core, width).transpose(1, 0, 2, 3)
    arranged = arranged.reshape(cols_n, pieces, piece_len, width)
    f32, bf16 = jnp.float32, jnp.bfloat16
    dma = pltpu.SemaphoreType.DMA
    out = pl.pallas_call(
        functools.partial(layer_kernel, states, rows_n, cols_n, share, per_core),
        in_specs=[pl.BlockSpec(memory_space=pltpu.VMEM)] * 8,
        out_specs=pl.BlockSpec(memory_space=pltpu.VMEM),
        out_shape=jax.ShapeDtypeStruct((cols_n, blocks // cols_n, block_len, width_out), bf16),
        scratch_shapes=[
            pltpu.VMEM((cols_n, pieces, piece_len, width), bf16),
            pltpu.VMEM((chunks, rows_n, cols_n, piece_len, width), bf16),
            pltpu.VMEM((chunks, chunk_len, tiles, LANES), bf16),
            pltpu.VMEM((chunks, chunk_len, tiles, LANES), bf16),
            pltpu.VMEM((chunk_len * tiles, LANES), f32),
            pltpu.VMEM((states, chunk_len + 8, LANES), f32),
            pltpu.VMEM((states, chunk_len + 8, LANES), f32),
            pltpu.VMEM((states, patches + 8, LANES), f32),
            pltpu.VMEM((states, patches + 8, LANES), f32),
            pltpu.VMEM((patches, inner), bf16),
            pltpu.VMEM((chunk_len * tiles, LANES), f32),
            pltpu.VMEM((chunk_len, inner), bf16),
            pltpu.VMEM((states * tiles, LANES), f32),
            pltpu.VMEM((states * tiles, LANES), f32),
            pltpu.VMEM((tiles, LANES), f32),
            pltpu.VMEM((blocks, block_len, width_out), bf16),
            pltpu.VMEM((cols_n, blocks // cols_n, block_len, width_out), bf16),
            pltpu.VMEM((per_core, states, tiles, LANES), f32),
            dma((pieces,)), dma((chunks,)), dma((cols_n,)), dma((cols_n,)),
            dma((chunks, group_n)), dma((chunks,)), dma((blocks,)),
            dma((cols_n, blocks // cols_n)),
        ],
        compiler_params=pltpu.CompilerParams(
            vmem_limit_bytes=VMEM_LIMIT, collective_id=0, has_side_effects=True
        ),
        name="layer",
    )(arranged, norm_gain[None], w_in, w_bc, rate_row, rate_col, skip_gain[None], w_out)
    out = out.reshape(cols_n, height, per_core, width_out).transpose(1, 0, 2, 3)
    return out.reshape(height, columns, width_out)


def solution(mesh):
    placed = (P(("slides", "cols"), "rows", None), P(), P(), P(), P(), P(), P(), P())
    return jax.shard_map(
        per_device,
        mesh=mesh,
        in_specs=placed,
        out_specs=P(("slides", "cols"), "rows", None),
        check_vma=False,
    )
```

time: 91.9 us -> 54.3 us (0.59); the launches traced: 90.1 us -> 54.1 us
  waiting for transfers between devices: 26.5 us -> 0 us
  Pallas kernels: 26.2 us -> 46.7 us
  starting transfers between devices: 14.7 us -> 0 us
  local copies, waits for them, and re-layouts: 14.7 us -> 7.35 us
  blocking collectives: 4.36 us -> 0 us
  matrix products: 3.35 us -> 0 us
    all_to_all x3 -> x0, waiting for transfers between devices: 26.5 us -> none  [the longest x1 14.8 us: per_device(): lax.all_to_all(row_mixed, ('rows', 'cols'), split_axis=1, concat_axis=0,...]
    pallas_call x2 -> x1, Pallas kernels: 26.2 us -> 46.7 us  [per_device(): pl.pallas_call(functools.partial(layer_kernel, states, rows_n, cols_n, sh...]
    all_to_all x3 -> x0, starting transfers between devices: 14.7 us -> none  [the longest x1 7.41 us: per_device(): lax.all_to_all(tokens, 'rows', split_axis=0, concat_axis=1, tiled=True)]
    all_to_all x1 -> x0, blocking collectives: 4.36 us -> none  [per_device(): lax.all_to_all(mixed, 'cols', split_axis=0, concat_axis=1, tiled=True)]
    convert_element_type x3 -> x0, local copies, waits for them, and re-layouts: 4.27 us -> none  [the longest x2 3.51 us: normalise(): as_float = tokens.astype(jnp.float32)]
    dot_general x2 -> x0, matrix products: 3.35 us -> none  [the longest x1 3 us: per_device(): jnp.dot(normed, w_in[:, inner:], preferred_element_type=jnp.float32)]
    reshape x2 -> x5, local copies, waits for them, and re-layouts: 2.16 us -> 5.39 us  [the longest x2 2.17 us: per_device(): tokens.reshape(height, cols_n, per_core, width).transpose(1, 0, 2, 3)]
    all_to_all x4 -> x0, local copies, waits for them, and re-layouts: 2.75 us -> none  [the longest x2 1.35 us: per_device(): lax.all_to_all(mixed, 'cols', split_axis=0, concat_axis=1, tiled=True)]
  transfers between devices with their start and end apart: 3 -> 0, of which waited for: 2 -> 0; matrix products, arithmetic and copies ran while one was open for 16% -> 0% of each run, Pallas kernels for 14% -> 0%
where the time goes in v2:
time: 54.3 us; the launch traced here: 54.1 us
  Pallas kernels  46.7 us (86%)
  local copies, waits for them, and re-layouts  7.35 us (14%)
    pallas_call x1, Pallas kernels, per_device(): pl.pallas_call(functools.partial(layer_kernel, states, rows_n, cols_n, sh...  46.7 us
    reshape x2, local copies, waits for them, and re-layouts, per_device(): tokens.reshape(height, cols_n, per_core, width).transpose(1, 0, 2, 3)  2.17 us
    unnamed x1, local copies, waits for them, and re-layouts  1.59 us
    reshape x1, local copies, waits for them, and re-layouts, per_device(): out = out.reshape(cols_n, height, per_core, width_out).transpose(1, 0, 2, 3)  1.24 us

profile of v2, /device:TPU:0, one launch (start us, length us, event | category | flops | bytes accessed | tf_op | source)
XLA Modules:
  0.0 54.1 jit_solution(3084954506169393981)
XLA Ops:
  0.0 1.6 %copy.10.wbc_ref = bf16[512,64]{1,0:T(8,128)(2,1)} copy(bf16[512,64]{0,1:T(8,128)(2,1)} %param.11) | data formatting | bytes 131072 | tf_op args[3]
  1.6 1.8 %reshape.12 = bf16[128,2,2,512]{3,2,1,0:T(2,128)(2,1)S(1)} reshape(bf16[128,4,512]{2,1,0:T(4,128)(2,1)} %param.8) | data formatting | bytes 1048576 | tf_op jit(solution)/shard_map/reshape | solution.py:318
  3.4 0.4 copy.13
  3.8 1.0 %reshape.13.tok_ref = bf16[2,32,8,512]{3,2,1,0:T(8,128)(2,1)} reshape(bf16[2,128,2,512]{3,2,1,0:T(2,128)(2,1)S(1)} %bitcast.8) | data formatting | bytes 1048576 | tf_op jit(solution)/shard_map/reshape | solution.py:319
  4.8 46.7 %layer.1 = bf16[2,2,128,512]{3,2,1,0:T(8,128)(2,1)} custom-call(bf16[2,32,8,512]{3,2,1,0:T(8,128)(2,1)} %reshape.13.tok_ref, f32[1,512]{1,0:T(1,128)} %bitcast.11, bf16[512,2048]{1,0:T(8,128)(2,1)} %win_ref.1, bf16[512,64]{1,0:T(8,128)(2,1)} %copy.10.wbc_ref, f32[16,1024]{1,0:T(8,128)} %rrate_ref.1, f32[16,1024]{1,0:T(8,128)} %crate_ref.1, ...), custom_call_target="tpu_custom_call" | custom-call | tf_op jit(solution)/shard_map/layer/pallas_call | solution.py:322
  51.5 1.2 %reshape.14 = bf16[2,128,2,512]{3,2,1,0:T(2,128)(2,1)S(1)} reshape(bf16[2,2,128,512]{3,2,1,0:T(8,128)(2,1)} %layer.1) | data formatting | bytes 1048576 | tf_op jit(solution)/shard_map/reshape | solution.py:355
  52.7 0.4 copy.11
  53.1 1.0 %reshape.15 = bf16[128,4,512]{2,1,0:T(4,128)(2,1)} reshape(bf16[128,2,2,512]{3,2,1,0:T(2,128)(2,1)S(1)} %copy.11) | data formatting | bytes 1048576 | tf_op jit(solution)/shard_map/reshape | solution.py:356

commit v3 on v2

--- a/solution.py
+++ b/solution.py
@@ -16,6 +16,10 @@
     as_float = tokens.astype(jnp.float32)
     scale_now = lax.rsqrt(jnp.mean(as_float * as_float, axis=-1, keepdims=True) + 1e-05)
     return (as_float * scale_now * gain).astype(jnp.bfloat16)
+
+
+def transposed_dot(a, b):
+    return lax.dot_general(a, b, (((1,), (1,)), ((), ())), preferred_element_type=jnp.float32)
 
 
 def spread_channels(ref, value, tiles):
@@ -47,16 +51,16 @@
 
 def layer_kernel(
     states, rows_n, cols_n, share, per_core,
-    tok_ref, gain_ref, win_ref, wbc_ref, rrate_ref, crate_ref, skip_ref, wout_ref,
+    tok_ref, gain_in, win_in, wbc_in, rrate_in, crate_in, skip_in, wout_in,
     out_ref,
-    tcol, tin, rsend, rrecv, u_ref, rb_ref, rc_ref, cb_ref, cc_ref, z_ref, y_ref, gated_ref,
+    gain_ref, win_ref, wbc_ref, rrate_ref, crate_ref, skip_ref, wout_ref, tcol, tin, rsend, rrecv, u_ref, rb_ref, rc_ref, cb_ref, cc_ref, z_ref, y_ref, gated_ref,
     rdecay, cdecay, skip_tile, stage, land, state_ref,
-    tsend_sem, tin_sem, csend_sem, crecv_sem, rsend_sem, rrecv_sem, osend_sem, orecv_sem,
+    tsend_sem, tin_sem, csend_sem, crecv_sem, rsend_sem, rrecv_sem, osend_sem, orecv_sem, fetch_sem,
 ):
     group_n = rows_n * cols_n
-    pieces = tok_ref.shape[1]
+    pieces = tok_ref.shape[0] // share
     chunks = tin.shape[0]
-    width = tok_ref.shape[3]
+    columns, width = tok_ref.shape[1:]
     inner = wout_ref.shape[0]
     tiles = inner // LANES
     piece_len = share * per_core
@@ -79,9 +83,15 @@
         return 0
 
     lax.fori_loop(0, group_n, greet, 0)
-    spread_channels(rdecay, jnp.exp(-rrate_ref[...]), tiles)
-    spread_channels(cdecay, jnp.exp(-crate_ref[...]), tiles)
-    spread_channels(skip_tile, skip_ref[...], tiles)
+    fetches = [
+        pltpu.make_async_copy(src, dst, fetch_sem.at[k])
+        for k, (src, dst) in enumerate((
+            (rrate_in, rrate_ref), (crate_in, crate_ref), (skip_in, skip_ref), (gain_in, gain_ref),
+            (wbc_in, wbc_ref), (tok_ref, tcol.at[c]), (win_in, win_ref), (wout_in, wout_ref),
+        ))
+    ]
+    for fetch in fetches:
+        fetch.start()
     pl.semaphore_wait(barrier, group_n - 1)
 
     local_chunks = max(1, chunks // cols_n)
@@ -95,7 +105,7 @@
     def token_copy(k):
         piece, q, g = piece_of(k)
         return g, pltpu.make_async_remote_copy(
-            src_ref=tok_ref.at[:, piece], dst_ref=tin.at[q, r],
+            src_ref=tok_ref.at[pl.ds(piece * share, share)], dst_ref=tin.at[q, r],
             send_sem=tsend_sem.at[piece], recv_sem=tin_sem.at[q],
             device_id=spot(g), device_id_type=MESH,
         )
@@ -105,7 +115,7 @@
 
         @pl.when(g == me)
         def _():
-            pltpu.make_async_copy(tok_ref.at[:, piece], tin.at[q, r], tin_sem.at[q]).start()
+            pltpu.make_async_copy(tok_ref.at[pl.ds(piece * share, share)], tin.at[q, r], tin_sem.at[q]).start()
 
         @pl.when(g != me)
         def _():
@@ -117,7 +127,7 @@
     def column_copy(step):
         other = (c + step) % cols_n
         return pltpu.make_async_remote_copy(
-            src_ref=tok_ref.at[other], dst_ref=tcol.at[c],
+            src_ref=tok_ref, dst_ref=tcol.at[c],
             send_sem=csend_sem.at[step], recv_sem=crecv_sem.at[step],
             device_id={"cols": other}, device_id_type=MESH,
         )
@@ -126,10 +136,14 @@
         column_copy(step).start()
 
     def gate_part(tokens, core):
-        normed = normalise(tokens.astype(jnp.float32).reshape(-1, width), gain_ref[...])
+        tokens = tokens.astype(jnp.float32)
+        own = tokens[:, :per_core]
+        for k in range(1, cols_n):
+            own = jnp.where(c == k, tokens[:, k * per_core : (k + 1) * per_core], own)
+        normed = normalise(own.reshape(-1, width), gain_ref[...])
         count = normed.shape[0]
         base = pl.multiple_of(core * count, count)
-        mixers = jnp.dot(normed, wbc_ref[...], preferred_element_type=jnp.float32)
+        mixers = transposed_dot(normed, wbc_ref[...])
         mixers = mixers.astype(jnp.bfloat16).astype(jnp.float32)
         spread_vectors(cb_ref, mixers, 2 * states, states, base)
         spread_vectors(cc_ref, mixers, 3 * states, states, base)
@@ -139,7 +153,12 @@
                 preferred_element_type=jnp.float32,
             ).astype(jnp.bfloat16)
 
-    gate_part(tok_ref[c], c)
+    for fetch in fetches:
+        fetch.wait()
+    spread_channels(rdecay, jnp.exp(-rrate_ref[...]), tiles)
+    spread_channels(cdecay, jnp.exp(-crate_ref[...]), tiles)
+    spread_channels(skip_tile, skip_ref[...], tiles)
+    gate_part(tcol[c], c)
 
     zero = jnp.zeros((tiles, LANES), jnp.float32)
     lanes = 2 if share % 2 == 0 else 1
@@ -156,7 +175,7 @@
     def row_chunk(q, _):
         pltpu.make_async_copy(tin.at[q], tin.at[q], tin_sem.at[q]).wait()
         normed = normalise(tin[q].astype(jnp.float32).reshape(chunk_len, width), gain_ref[...])
-        mixers = jnp.dot(normed, wbc_ref[...], preferred_element_type=jnp.float32)
+        mixers = transposed_dot(normed, wbc_ref[...])
         mixers = mixers.astype(jnp.bfloat16).astype(jnp.float32)
         spread_vectors(rb_ref, mixers, 0, states, 0)
         spread_vectors(rc_ref, mixers, states, states, 0)
@@ -172,16 +191,18 @@
         def one_group(first, _):
             def one_step(j, carry):
                 carry = list(carry)
-                for w in range(per_core):
+                for w in range(columns):
                     for b in range(lanes):
-                        patch = (j * share + first * lanes + b) * per_core + w
+                        row = first * lanes + b
+                        patch = (j * share + row) * columns + w
+                        owner = j * cols_n + w // per_core
                         value = u_ref[pl.ds(pl.multiple_of(patch * tiles, tiles), tiles), :]
                         carry[b], total = scan_step(carry[b], decay, value, rb_ref, rc_ref,
                                                     patch, skip * value, tiles)
-                        rsend[q, patch] = total.astype(jnp.bfloat16)
+                        rsend[q, (owner * share + row) * per_core + w % per_core] = total.astype(jnp.bfloat16)
                 return tuple(carry)
 
-            lax.fori_loop(0, group_n, one_step, tuple((zero,) * states for _ in range(lanes)))
+            lax.fori_loop(0, rows_n, one_step, tuple((zero,) * states for _ in range(lanes)))
             return 0
 
         lax.fori_loop(0, share // lanes, one_group, 0)
@@ -295,7 +316,13 @@
                 pltpu.make_async_copy(
                     land.at[source, i], land.at[source, i], orecv_sem.at[source, i]
                 ).wait()
-    out_ref[...] = land[...]
+    for i in range(blocks_home):
+        parts = [
+            land[s, i].astype(jnp.float32).reshape(block_len // per_core, per_core, -1)
+            for s in range(cols_n)
+        ]
+        rows = block_len // per_core
+        out_ref[i * rows : (i + 1) * rows] = jnp.concatenate(parts, axis=1).astype(jnp.bfloat16)
 
 
 def per_device(tokens, norm_gain, w_in, w_bc, rate_row, rate_col, skip_gain, w_out):
@@ -306,7 +333,7 @@
     group_n = rows_n * cols_n
     per_core = columns // cols_n
     total = height * cols_n
-    share = min(4, total // group_n)
+    share = min(2, total // group_n)
     chunks = total // (group_n * share)
     pieces = height // share
     piece_len = share * per_core
@@ -315,18 +342,23 @@
     blocks = max(chunks, cols_n)
     block_len = total * per_core // blocks
     patches = total * per_core
-    arranged = tokens.reshape(height, cols_n, per_core, width).transpose(1, 0, 2, 3)
-    arranged = arranged.reshape(cols_n, pieces, piece_len, width)
     f32, bf16 = jnp.float32, jnp.bfloat16
     dma = pltpu.SemaphoreType.DMA
     out = pl.pallas_call(
         functools.partial(layer_kernel, states, rows_n, cols_n, share, per_core),
-        in_specs=[pl.BlockSpec(memory_space=pltpu.VMEM)] * 8,
+        in_specs=[pl.BlockSpec(memory_space=pl.ANY)] * 8,
         out_specs=pl.BlockSpec(memory_space=pltpu.VMEM),
-        out_shape=jax.ShapeDtypeStruct((cols_n, blocks // cols_n, block_len, width_out), bf16),
+        out_shape=jax.ShapeDtypeStruct((height, columns, width_out), bf16),
         scratch_shapes=[
-            pltpu.VMEM((cols_n, pieces, piece_len, width), bf16),
-            pltpu.VMEM((chunks, rows_n, cols_n, piece_len, width), bf16),
+            pltpu.VMEM((1, width), f32),
+            pltpu.VMEM(w_in.shape, bf16),
+            pltpu.VMEM(w_bc.shape[::-1], bf16),
+            pltpu.VMEM(rate_row.shape, f32),
+            pltpu.VMEM(rate_col.shape, f32),
+            pltpu.VMEM((1, inner), f32),
+            pltpu.VMEM(w_out.shape, bf16),
+            pltpu.VMEM((cols_n, height, columns, width), bf16),
+            pltpu.VMEM((chunks, rows_n, share, columns, width), bf16),
             pltpu.VMEM((chunks, chunk_len, tiles, LANES), bf16),
             pltpu.VMEM((chunks, chunk_len, tiles, LANES), bf16),
             pltpu.VMEM((chunk_len * tiles, LANES), f32),
@@ -345,15 +377,14 @@
             pltpu.VMEM((per_core, states, tiles, LANES), f32),
             dma((pieces,)), dma((chunks,)), dma((cols_n,)), dma((cols_n,)),
             dma((chunks, group_n)), dma((chunks,)), dma((blocks,)),
-            dma((cols_n, blocks // cols_n)),
+            dma((cols_n, blocks // cols_n)), dma((8,)),
         ],
         compiler_params=pltpu.CompilerParams(
             vmem_limit_bytes=VMEM_LIMIT, collective_id=0, has_side_effects=True
         ),
         name="layer",
-    )(arranged, norm_gain[None], w_in, w_bc, rate_row, rate_col, skip_gain[None], w_out)
-    out = out.reshape(cols_n, height, per_core, width_out).transpose(1, 0, 2, 3)
-    return out.reshape(height, columns, width_out)
+    )(tokens, norm_gain[None], w_in, w_bc.T, rate_row, rate_col, skip_gain[None], w_out)
+    return out
 
 
 def solution(mesh):

time: 54.3 us -> 50.7 us (0.934)
  local copies, waits for them, and re-layouts: 7.35 us -> 2.02 us
  Pallas kernels: 46.7 us -> 48.5 us
    reshape x5 -> x0, local copies, waits for them, and re-layouts: 5.39 us -> none  [the longest x2 2.17 us: per_device(): tokens.reshape(height, cols_n, per_core, width).transpose(1, 0, 2, 3)]
    pallas_call x1, Pallas kernels: 46.7 us -> 48.5 us  [per_device(): pl.pallas_call(functools.partial(layer_kernel, states, rows_n, cols_n, sh...]
where the time goes in v3:
time: 50.7 us; the launch traced here: 50.5 us
  Pallas kernels  48.5 us (96%)
  local copies, waits for them, and re-layouts  2.02 us (4%)
    pallas_call x1, Pallas kernels, per_device(): pl.pallas_call(functools.partial(layer_kernel, states, rows_n, cols_n, sh...  48.5 us
    unnamed x1, local copies, waits for them, and re-layouts  2.02 us

profile of v3, /device:TPU:0, one launch (start us, length us, event | category | flops | bytes accessed | tf_op | source)
XLA Modules:
  0.0 50.5 jit_solution(6651333910416812842)
XLA Ops:
  0.0 48.5 %layer.1 = bf16[128,4,512]{2,1,0:T(4,128)(2,1)} custom-call(bf16[128,4,512]{2,1,0:T(4,128)(2,1)} %tok_ref.1, f32[1,512]{1,0:T(1,128)} %bitcast.5, bf16[512,2048]{1,0:T(8,128)(2,1)} %win_in.1, bf16[64,512]{1,0:T(8,128)(2,1)} %bitcast.3, f32[16,1024]{1,0:T(8,128)} %rrate_in.1, f32[16,1024]{1,0:T(8,128)} %crate_in.1, f32[1,1024]{1,0:T(1,128)} %bitcast.4, ...), custom_call_target="tpu_custom_call" | custom-call | tf_op jit(solution)/shard_map/layer/pallas_call | solution.py:347
  48.5 2.0 %copy.10 = bf16[128,4,512]{2,1,0:T(4,128)(2,1)} copy(bf16[128,4,512]{2,1,0:T(4,128)(2,1)} %layer.1) | data formatting | bytes 1048576

commit v4 on v3

--- a/solution.py
+++ b/solution.py
@@ -333,7 +333,7 @@
     group_n = rows_n * cols_n
     per_core = columns // cols_n
     total = height * cols_n
-    share = min(2, total // group_n)
+    share = min(4, total // group_n)
     chunks = total // (group_n * share)
     pieces = height // share
     piece_len = share * per_core

time: 50.7 us -> 47.7 us (0.941)
  Pallas kernels: 48.5 us -> 45.5 us
    pallas_call x1, Pallas kernels: 48.5 us -> 45.5 us  [per_device(): pl.pallas_call(functools.partial(layer_kernel, states, rows_n, cols_n, sh...]
where the time goes in v4:
time: 47.7 us; the launch traced here: 47.5 us
  Pallas kernels  45.5 us (95%)
  local copies, waits for them, and re-layouts  2.02 us (4%)
    pallas_call x1, Pallas kernels, per_device(): pl.pallas_call(functools.partial(layer_kernel, states, rows_n, cols_n, sh...  45.5 us
    unnamed x1, local copies, waits for them, and re-layouts  2.02 us

profile of v4, /device:TPU:0, one launch (start us, length us, event | category | flops | bytes accessed | tf_op | source)
XLA Modules:
  0.0 47.5 jit_solution(5799739382262883145)
XLA Ops:
  0.0 45.5 %layer.1 = bf16[128,4,512]{2,1,0:T(4,128)(2,1)} custom-call(bf16[128,4,512]{2,1,0:T(4,128)(2,1)} %tok_ref.1, f32[1,512]{1,0:T(1,128)} %bitcast.5, bf16[512,2048]{1,0:T(8,128)(2,1)} %win_in.1, bf16[64,512]{1,0:T(8,128)(2,1)} %bitcast.3, f32[16,1024]{1,0:T(8,128)} %rrate_in.1, f32[16,1024]{1,0:T(8,128)} %crate_in.1, f32[1,1024]{1,0:T(1,128)} %bitcast.4, ...), custom_call_target="tpu_custom_call" | custom-call | tf_op jit(solution)/shard_map/layer/pallas_call | solution.py:347
  45.5 2.0 %copy.10 = bf16[128,4,512]{2,1,0:T(4,128)(2,1)} copy(bf16[128,4,512]{2,1,0:T(4,128)(2,1)} %layer.1) | data formatting | bytes 1048576
